TPU v7x, 32 devices: a whole 2x2x4 slice. The times are simulated.
32 devices in a mesh: tile: 4 (over x, core), blk: 8 (over z, y).
Axes of the slice: x: 2, y: 2, z: 4, core: 2. Of those that a mesh axis runs over, the one named last changes fastest.
Arguments:
- tokens: bfloat16 [32768, 384], P(('tile', 'blk')), may hold values from -52 to 52
- ln_gain: float32 [384], replicated, may hold values from 0.1 to 1.9
- route: int32 [32768, 2], P(('tile', 'blk')), may hold values from 0 to 15, all different within a row; in each aligned block of 1024 rows (0 to 1023, 1024 to 2047, ...) at most 192 rows name the same one
- gates: float32 [32768, 2], P(('tile', 'blk')), may hold values from 0.1 to 1
- w_gate: bfloat16 [16, 384, 1024], P('tile', 'blk'), may hold values from -0.3125 to 0.3125
- w_up: bfloat16 [16, 384, 1024], P('tile', 'blk'), may hold values from -0.3125 to 0.3125
- w_down: bfloat16 [16, 1024, 384], P('tile', 'blk'), may hold values from -0.1875 to 0.1875
- d_mixed: bfloat16 [32768, 384], P(('tile', 'blk')), may hold values from -6 to 6
Outputs:
- mixed: bfloat16 [32768, 384], P(('tile', 'blk'))
- grad_gates: float32 [32768, 2], P(('tile', 'blk'))
- grad_tokens: bfloat16 [32768, 384], P(('tile', 'blk'))
- grad_w_gate: float32 [16, 384, 1024], P('tile', 'blk')
- grad_w_up: float32 [16, 384, 1024], P('tile', 'blk')
- grad_w_down: float32 [16, 1024, 384], P('tile', 'blk')
Inputs may be any that keep to these rules, and one draw needn't show every extreme that they name: `route`: each row names 2 different experts; within the rows of one device no expert is named more than 192 times, a bound that some block reaches.
All inputs are finite; a program needn't handle non-finite values.
Results may differ from a plain program's by a relative error of at most 0.014.
Values may be sent and summed in bfloat16 or wider, within the bound.
A program may use at most 192 MiB of HBM per device.

v0:
```python
import jax
import jax.numpy as jnp
from jax import lax
from jax.sharding import PartitionSpec as P


def layer_norm(values, ln_gain):
    centre = jnp.mean(values, axis=-1, keepdims=True)
    centred = values - centre
    spread = jnp.mean(centred * centred, axis=-1, keepdims=True)
    return values * lax.rsqrt(spread + 1e-05) * ln_gain


def expert_forward(inputs_rows, weight_gate, weight_up, weight_down):
    gate_pre = jnp.einsum(
        "erd,edh->erh", inputs_rows, weight_gate, preferred_element_type=jnp.float32
    )
    up_pre = jnp.einsum("erd,edh->erh", inputs_rows, weight_up, preferred_element_type=jnp.float32)
    sigma_gate = jax.nn.sigmoid(gate_pre)
    hidden_act = (gate_pre * sigma_gate * up_pre).astype(jnp.bfloat16)
    expert_rows = jnp.einsum(
        "erh,ehd->erd", hidden_act, weight_down, preferred_element_type=jnp.float32
    )
    return (expert_rows.astype(jnp.bfloat16), gate_pre, up_pre, hidden_act)


def expert_backward(
    inputs_rows, d_rows, gate_pre, up_pre, hidden_act, weight_gate, weight_up, weight_down
):
    d_act = jnp.einsum("erd,ehd->erh", d_rows, weight_down, preferred_element_type=jnp.float32)
    sigma_gate = jax.nn.sigmoid(gate_pre)
    d_gate = (d_act * up_pre * sigma_gate * (1.0 + gate_pre * (1.0 - sigma_gate))).astype(
        jnp.bfloat16
    )
    d_up = (d_act * gate_pre * sigma_gate).astype(jnp.bfloat16)
    d_in = jnp.einsum(
        "erh,edh->erd", d_gate, weight_gate, preferred_element_type=jnp.float32
    ) + jnp.einsum("erh,edh->erd", d_up, weight_up, preferred_element_type=jnp.float32)
    grad_gate = jnp.einsum("erd,erh->edh", inputs_rows, d_gate, preferred_element_type=jnp.float32)
    grad_up = jnp.einsum("erd,erh->edh", inputs_rows, d_up, preferred_element_type=jnp.float32)
    grad_down = jnp.einsum("erh,erd->ehd", hidden_act, d_rows, preferred_element_type=jnp.float32)
    return (d_in.astype(jnp.bfloat16), grad_gate, grad_up, grad_down)


def on_device(tokens, ln_gain, route, gates, w_gate, w_up, w_down, d_mixed):
    tok_rows, features = tokens.shape
    top_picks = route.shape[1]
    per_tile = w_gate.shape[0]
    tile_count = lax.axis_size("tile")
    experts_all = per_tile * tile_count
    capacity = max(2, 3 * tok_rows * top_picks // (2 * experts_all))
    tokens_wide = tokens.astype(jnp.float32)
    normed = layer_norm(tokens_wide, ln_gain).astype(jnp.bfloat16)
    flat_route = route.reshape(-1)
    onehot = (flat_route[:, None] == lax.iota(jnp.int32, experts_all)[None, :]).astype(jnp.int32)
    slot_rank = jnp.sum((jnp.cumsum(onehot, axis=0) - 1) * onehot, axis=1)
    slot_index = flat_route * capacity + slot_rank

    def pack_slots(values):
        blank = jnp.zeros((experts_all * capacity, features), jnp.bfloat16)
        return blank.at[slot_index].set(values).reshape(tile_count, per_tile, capacity, features)

    def to_experts(packed):
        arrived = lax.all_to_all(packed, "tile", split_axis=0, concat_axis=2, tiled=True)[0]
        return arrived

    def from_experts(results):
        returned = lax.all_to_all(results[None], "tile", split_axis=2, concat_axis=0, tiled=True)
        picked = returned.reshape(experts_all * capacity, features)[slot_index]
        return picked.reshape(tok_rows, top_picks, features).astype(jnp.float32)

    weight_gate, weight_up, weight_down = (
        lax.all_gather(w_gate, "blk", axis=1, tiled=True),
        lax.all_gather(w_up, "blk", axis=1, tiled=True),
        lax.all_gather(w_down, "blk", axis=1, tiled=True),
    )
    inputs_rows = to_experts(pack_slots(jnp.repeat(normed, top_picks, axis=0)))
    expert_rows, gate_pre, up_pre, hidden_act = expert_forward(
        inputs_rows, weight_gate, weight_up, weight_down
    )
    expert_out = from_experts(expert_rows)
    mixed = jnp.sum(gates[:, :, None] * expert_out, axis=1).astype(jnp.bfloat16)
    d_wide = d_mixed.astype(jnp.float32)
    grad_gates = jnp.sum(d_wide[:, None, :] * expert_out, axis=-1)
    d_out = (
        (gates[:, :, None] * d_wide[:, None, :])
        .astype(jnp.bfloat16)
        .reshape(tok_rows * top_picks, features)
    )
    d_rows = to_experts(pack_slots(d_out))
    d_in, grad_gate, grad_up, grad_down = expert_backward(
        inputs_rows, d_rows, gate_pre, up_pre, hidden_act, weight_gate, weight_up, weight_down
    )
    d_normed = jnp.sum(from_experts(d_in), axis=1)

    def normalize(values):
        return layer_norm(values, ln_gain)

    unused, pullback = jax.vjp(normalize, tokens_wide)
    grad_tokens = pullback(d_normed)[0].astype(jnp.bfloat16)
    total_gate, total_up, total_down = (
        lax.psum_scatter(
            grad_gate.astype(jnp.bfloat16), "blk", scatter_dimension=1, tiled=True
        ).astype(jnp.float32),
        lax.psum_scatter(
            grad_up.astype(jnp.bfloat16), "blk", scatter_dimension=1, tiled=True
        ).astype(jnp.float32),
        lax.psum_scatter(
            grad_down.astype(jnp.bfloat16), "blk", scatter_dimension=1, tiled=True
        ).astype(jnp.float32),
    )
    return (mixed, grad_gates, grad_tokens, total_gate, total_up, total_down)


def solution(mesh):
    placed = (
        P(("tile", "blk"), None),
        P(),
        P(("tile", "blk"), None),
        P(("tile", "blk"), None),
        P("tile", "blk", None),
        P("tile", "blk", None),
        P("tile", "blk", None),
        P(("tile", "blk"), None),
    )
    return jax.shard_map(
        on_device,
        mesh=mesh,
        in_specs=placed,
        out_specs=(
            P(("tile", "blk"), None),
            P(("tile", "blk"), None),
            P(("tile", "blk"), None),
            P("tile", "blk", None),
            P("tile", "blk", None),
            P("tile", "blk", None),
        ),
        check_vma=False,
    )
```

profile of v0, /device:TPU:0, one launch (start us, length us, event | category | flops | bytes accessed | tf_op | source)
XLA Modules:
  0.0 456.5 jit_solution(16825820951956494859)
XLA Ops:
  20.1 11.6 %scatter_custom_fusion = bf16[3072,384]{1,0:T(8,128)(2,1)} fusion(s32[2048]{0:T(1024)S(1)} %bitcast.70, bf16[2048,384]{1,0:T(8,128)(2,1)} %reshape.153, bf16[]{:T(256)} %constant.10.clone.1), kind=kCustom, calls=%fused_computation.35 | custom fusion | bytes 2359808 | tf_op jit(solution)/shard_map/scatter | solution.py:61
  42.5 5.3 %mul.150 = f32[2048,384]{1,0:T(8,128)} reshape(f32[1024,2,384]{2,1,0:T(2,128)} %mul.146) | data formatting | bytes 6291456 | tf_op jit(solution)/shard_map/mul | solution.py:84
  47.8 12.6 %scatter_custom_fusion.1 = bf16[3072,384]{1,0:T(8,128)(2,1)} fusion(s32[2048]{0:T(1024)S(1)} %bitcast.71, f32[2048,384]{1,0:T(8,128)} %mul.150, f32[2048]{0:T(1024)S(1)} %mul.148, bf16[]{:T(256)} %constant.10.clone.1), kind=kCustom, calls=%fused_computation.32 | custom fusion | flops 1572864 | bytes 5513218 | tf_op jit(solution)/shard_map/scatter | solution.py:61
  73.1 26.4 %all-to-all-done.2 = bf16[4,4,192,384]{3,2,1,0:T(8,128)(2,1)} async-done(((bf16[4,4,192,384]{3,2,1,0:T(8,128)(2,1)}), bf16[4,4,192,384]{3,2,1,0:T(8,128)(2,1)}, u32[]{:S(2)}, u32[]{:S(2)}) %all-to-all-start.2) | async-done | bytes 2359328 | tf_op jit(solution)/shard_map/all_to_all | solution.py:64
  102.9 8.5 %fusion.21 = f32[4,768,1024]{2,1,0:T(8,128)} fusion(bf16[4,768,384]{2,1,0:T(8,128)(2,1)S(1)} %bitcast.58, bf16[4,384,1024]{2,1,0:T(8,128)(2,1)} %all-gather.4.cloned.1.call-done), kind=kOutput, calls=%fused_computation.53 | convolution fusion | flops 2415919104 | bytes 18087936 | tf_op jit(solution)/shard_map/erd,edh->erh/dot_general | solution.py:15
  111.4 22.5 %all-gather.6.cloned.1.call-done = bf16[4,384,1024]{2,1,0:T(8,128)(2,1)} async-done(((bf16[4,48,1024]{2,1,0:T(8,128)(2,1)}), bf16[4,384,1024]{2,1,0:T(8,128)(2,1)}) %all-gather.6.cloned.1.call-update) | async-done | bytes 3145744 | tf_op jit(solution)/shard_map/all_gather | solution.py:74
  133.9 8.3 %fusion.22 = f32[4,768,1024]{2,1,0:T(8,128)} fusion(bf16[4,768,384]{2,1,0:T(8,128)(2,1)S(1)} %bitcast.59, bf16[4,384,1024]{2,1,0:T(8,128)(2,1)} %all-gather.6.cloned.1.call-done), kind=kOutput, calls=%fused_computation.54 | convolution fusion | flops 2415919104 | bytes 18087936 | tf_op jit(solution)/shard_map/erd,edh->erh/dot_general | solution.py:18
  142.2 52.6 %all-gather.8.cloned.1.call-done = bf16[4,1024,384]{2,1,0:T(8,128)(2,1)} async-done(((bf16[4,128,384]{2,1,0:T(8,128)(2,1)}), bf16[4,1024,384]{2,1,0:T(8,128)(2,1)}) %all-gather.8.cloned.1.call-update) | async-done | bytes 3145744 | tf_op jit(solution)/shard_map/all_gather | solution.py:75
  194.8 18.0 %multiply_convert_fusion = (bf16[4,768,1024]{2,1,0:T(8,128)(2,1)}, bf16[4,768,1024]{2,1,0:T(8,128)(2,1)}, bf16[4,768,1024]{2,1,0:T(8,128)(2,1)}) fusion(f32[4,768,1024]{2,1,0:T(8,128)} %fusion.21, f32[4,768,1024]{2,1,0:T(8,128)} %fusion.22, bf16[4,768,384]{2,1,0:T(8,128)(2,1)} %bitcast.66, bf16[4,1024,384]{2,1,0:T(8,128)(2,1)} %all-gather.8.cloned.1.call-done), kind=kOutput, calls=%fused_computation.4 | convolution fusion | flops 2466250752 | bytes 49545216 | tf_op jit(solution)/shard_map/erd,ehd->erh/dot_general | solution.py:30
  212.8 7.1 %convolution_convert_fusion.2 = bf16[4,384,1024]{2,1,0:T(8,128)(2,1)} fusion(bf16[4,768,384]{2,1,0:T(8,128)(2,1)S(1)} %bitcast.60, bf16[4,768,1024]{2,1,0:T(8,128)(2,1)} %get-tuple-element.15), kind=kOutput, calls=%fused_computation.20 | convolution fusion | flops 2417491968 | bytes 11796480 | tf_op jit(solution)/shard_map/erd,erh->edh/dot_general | solution.py:39
  220.4 7.1 %convolution_convert_fusion.1 = bf16[4,384,1024]{2,1,0:T(8,128)(2,1)} fusion(bf16[4,768,384]{2,1,0:T(8,128)(2,1)S(1)} %bitcast.61, bf16[4,768,1024]{2,1,0:T(8,128)(2,1)} %get-tuple-element.14), kind=kOutput, calls=%fused_computation.19 | convolution fusion | flops 2417491968 | bytes 11796480 | tf_op jit(solution)/shard_map/erd,erh->edh/dot_general | solution.py:40
  229.2 8.0 %convolution_convert_fusion = bf16[4,1024,384]{2,1,0:T(8,128)(2,1)} fusion(bf16[4,768,1024]{2,1,0:T(8,128)(2,1)} %get-tuple-element.16, bf16[4,768,384]{2,1,0:T(8,128)(2,1)S(1)} %bitcast.67), kind=kOutput, calls=%fused_computation.18 | convolution fusion | flops 2417491968 | bytes 11796480 | tf_op jit(solution)/shard_map/erh,erd->ehd/dot_general | solution.py:41
  237.2 6.7 %fusion.23 = f32[4,768,384]{2,1,0:T(8,128)S(1)} fusion(bf16[4,768,1024]{2,1,0:T(8,128)(2,1)} %get-tuple-element.15, bf16[4,384,1024]{2,1,0:T(8,128)(2,1)} %all-gather.4.cloned.1.call-done), kind=kOutput, calls=%fused_computation.55 | convolution fusion | flops 2415919104 | bytes 14155776 | tf_op jit(solution)/shard_map/erh,edh->erd/dot_general | solution.py:36
  254.6 7.2 %convert_bitcast_fusion = bf16[1,4,768,384]{3,2,1,0:T(8,128)(2,1)S(1)} fusion(bf16[4,768,1024]{2,1,0:T(8,128)(2,1)} %get-tuple-element.16, bf16[4,1024,384]{2,1,0:T(8,128)(2,1)} %all-gather.8.cloned.1.call-done), kind=kOutput, calls=%fused_computation.17 | convolution fusion | flops 2417098752 | bytes 11796480 | tf_op jit(solution)/shard_map/erh,ehd->erd/dot_general | solution.py:21
  265.1 18.0 %all-to-all-done.3 = bf16[1,4,768,384]{3,1,0,2:T(4,128)(2,1)S(1)} async-done(((bf16[1,4,768,384]{3,1,0,2:T(4,128)(2,1)}), bf16[1,4,768,384]{3,1,0,2:T(4,128)(2,1)S(1)}, u32[]{:S(2)}, u32[]{:S(2)}) %all-to-all-start.3) | async-done | bytes 2359328 | tf_op jit(solution)/shard_map/all_to_all | solution.py:68
  292.1 9.0 %gather_fusion.1 = bf16[2048,384]{1,0:T(8,128)(2,1)} fusion(bf16[3072,384]{1,0:T(8,128)(2,1)S(1)} %bitcast.57, s32[2048]{0:T(1024)S(1)} %broadcast_clamp_fusion), kind=kCustom, calls=%fused_computation.1 | custom fusion | bytes 3153920 | tf_op jit(solution)/shard_map/gather | solution.py:69
  301.2 4.9 %reshape.132 = f32[1024,2,384]{2,1,0:T(2,128)} reshape(bf16[2048,384]{1,0:T(8,128)(2,1)} %gather_fusion.1) | data formatting | bytes 4718592 | tf_op jit(solution)/shard_map/convert_element_type | solution.py:70
  306.0 11.6 %all-to-all-done.1 = bf16[1,4,768,384]{3,1,0,2:T(4,128)(2,1)} async-done(((bf16[1,4,768,384]{3,1,0,2:T(4,128)(2,1)}), bf16[1,4,768,384]{3,1,0,2:T(4,128)(2,1)}, u32[]{:S(2)}, u32[]{:S(2)}) %all-to-all-start.1) | async-done | bytes 2359328 | tf_op jit(solution)/shard_map/all_to_all | solution.py:68
  319.7 9.1 %gather_fusion = bf16[2048,384]{1,0:T(8,128)(2,1)} fusion(bf16[3072,384]{1,0:T(8,128)(2,1)S(1)} %bitcast.56, s32[2048]{0:T(1024)S(1)} %broadcast_clamp_fusion), kind=kCustom, calls=%fused_computation | custom fusion | bytes 3153920 | tf_op jit(solution)/shard_map/gather | solution.py:69
  328.8 5.0 %reshape.131 = f32[1024,2,384]{2,1,0:T(2,128)} reshape(bf16[2048,384]{1,0:T(8,128)(2,1)} %gather_fusion) | data formatting | bytes 4718592 | tf_op jit(solution)/shard_map/convert_element_type | solution.py:70
  333.8 10.1 %multiply_reduce_fusion = (f32[1024,2]{1,0:T(8,128)S(1)}, bf16[1024,384]{1,0:T(8,128)(2,1)}) fusion(f32[1024,2,384]{2,1,0:T(2,128)} %reshape.131, f32[1024,384]{1,0:T(8,128)S(1)} %copy-done.4, f32[1024,2]{1,0:T(8,128)S(1)} %copy-done.5), kind=kLoop, calls=%fused_computation.10 | loop fusion | flops 2750464 | bytes 5521408 | tf_op jit(solution)/shard_map/reduce_sum | solution.py:84
  344.7 5.7 %reduce_sum.96 = f32[1024,384]{1,0:T(8,128)S(1)} reduce(f32[1024,2,384]{2,1,0:T(2,128)} %reshape.132, f32[]{:T(128)} %constant.25.clone.1), dimensions={1}, to_apply=%region_9.10 | reduce | flops 393216 | bytes 4718596 | tf_op jit(solution)/shard_map/reduce_sum | solution.py:94
  355.0 15.5 %reduce-scatter.6.cloned.1.call-done = bf16[4,48,1024]{2,1,0:T(8,128)(2,1)} async-done(((bf16[4,384,1024]{2,1,0:T(8,128)(2,1)}), bf16[4,48,1024]{2,1,0:T(8,128)(2,1)}) %reduce-scatter.6.cloned.1.call-update) | async-done | bytes 393232 | tf_op jit(solution)/shard_map/reduce_scatter | solution.py:105
  372.5 75.0 %reduce-scatter.8.cloned.1.call-done = bf16[4,128,384]{2,1,0:T(8,128)(2,1)} async-done(((bf16[4,1024,384]{2,1,0:T(8,128)(2,1)}), bf16[4,128,384]{2,1,0:T(8,128)(2,1)}) %reduce-scatter.8.cloned.1.call-update) | async-done | bytes 393232 | tf_op jit(solution)/shard_map/reduce_scatter | solution.py:108
  (87 shorter events, 76.1 us)
Async XLA Ops:
  7.2 8.7 %copy-start = (bf16[1024,384]{1,0:T(8,128)(2,1)S(1)}, bf16[1024,384]{1,0:T(8,128)(2,1)}, u32[]{:S(2)}) copy-start(bf16[1024,384]{1,0:T(8,128)(2,1)} %param.8) | copy-start | bytes 2359300
  7.2 9.4 %copy-start.9 = (f32[384]{0:T(512)S(1)}, f32[384]{0:T(512)}, u32[]{:S(2)}) copy-start(f32[384]{0:T(512)} %param.9) | copy-start | bytes 4612
  7.2 95.7 %all-gather.4.cloned.1.call-start = ((), (), s32[]{:S(2)}) async-start(), calls=%async_computation.7 | async-start | bytes 3538944 | tf_op jit(solution)/shard_map/all_gather | solution.py:73
  7.9 126.0 %all-gather.6.cloned.1.call-start = ((), (), s32[]{:S(2)}) async-start(), calls=%async_computation.8 | async-start | bytes 3538944 | tf_op jit(solution)/shard_map/all_gather | solution.py:74
  8.7 186.1 %all-gather.8.cloned.1.call-start = ((), (), s32[]{:S(2)}) async-start(), calls=%async_computation.9 | async-start | bytes 3538944 | tf_op jit(solution)/shard_map/all_gather | solution.py:75
  10.3 6.5 %copy-start.8 = (s32[1024,2]{0,1:T(2,128)S(1)}, s32[1024,2]{0,1:T(2,128)}, u32[]{:S(2)}) copy-start(s32[1024,2]{0,1:T(2,128)} %param.10) | copy-start | bytes 24580
  31.7 4.8 %copy-start.10 = (f32[1024,2]{0,1:T(2,128)S(1)}, f32[1024,2]{0,1:T(2,128)}, u32[]{:S(2)}) copy-start(f32[1024,2]{0,1:T(2,128)} %param.11) | copy-start | bytes 24580
  31.7 33.4 %all-to-all-start = ((bf16[4,4,192,384]{3,2,1,0:T(8,128)(2,1)}), bf16[4,4,192,384]{3,2,1,0:T(8,128)(2,1)S(1)}, u32[]{:S(2)}, u32[]{:S(2)}) async-start(bf16[4,4,192,384]{3,2,1,0:T(8,128)(2,1)} %bitcast.65), calls=%async_computation | async-start | bytes 4718592 | tf_op jit(solution)/shard_map/all_to_all | solution.py:64
  65.1 1.4 copy-start.1
  66.5 33.0 %all-to-all-start.2 = ((bf16[4,4,192,384]{3,2,1,0:T(8,128)(2,1)}), bf16[4,4,192,384]{3,2,1,0:T(8,128)(2,1)}, u32[]{:S(2)}, u32[]{:S(2)}) async-start(bf16[4,4,192,384]{3,2,1,0:T(8,128)(2,1)} %bitcast.64), calls=%async_computation.2 | async-start | bytes 4718592 | tf_op jit(solution)/shard_map/all_to_all | solution.py:64
  71.0 281.9 %reduce-scatter.4.cloned.1.call-start = ((), (), s32[]{:S(2)}) async-start(), calls=%async_computation.10 | async-start | bytes 3538944 | tf_op jit(solution)/shard_map/reduce_scatter | solution.py:102
  219.9 150.6 %reduce-scatter.6.cloned.1.call-start = ((), (), s32[]{:S(2)}) async-start(), calls=%async_computation.11 | async-start | bytes 3538944 | tf_op jit(solution)/shard_map/reduce_scatter | solution.py:105
  227.5 1.7 copy-start.7
  227.6 220.0 %reduce-scatter.8.cloned.1.call-start = ((), (), s32[]{:S(2)}) async-start(), calls=%async_computation.12 | async-start | bytes 3538944 | tf_op jit(solution)/shard_map/reduce_scatter | solution.py:108
  237.2 6.8 %slice-start = ((s8[6291456]{0:T(1024)(128)(4,1)}), s8[2097152]{0:T(1024)(128)(4,1)S(1)}, s32[]{:S(2)}) async-start(s8[6291456]{0:T(1024)(128)(4,1)} %bitcast.74), calls=%async_computation.13 | async-start | bytes 4194304
  237.2 6.7 %copy-start.6 = (bf16[4,384,1024]{2,1,0:T(8,128)(2,1)S(1)}, bf16[4,384,1024]{2,1,0:T(8,128)(2,1)}, u32[]{:S(2)}) copy-start(bf16[4,384,1024]{2,1,0:T(8,128)(2,1)} %all-gather.6.cloned.1.call-done) | copy-start | bytes 9437188
  237.2 6.8 %slice-start.1 = ((s8[6291456]{0:T(1024)(128)(4,1)}), s8[4194304]{0:T(1024)(128)(4,1)S(1)}, s32[]{:S(2)}) async-start(s8[6291456]{0:T(1024)(128)(4,1)} %bitcast.74), calls=%async_computation.14 | async-start | bytes 8388608
  251.0 32.1 %all-to-all-start.3 = ((bf16[1,4,768,384]{3,1,0,2:T(4,128)(2,1)}), bf16[1,4,768,384]{3,1,0,2:T(4,128)(2,1)S(1)}, u32[]{:S(2)}, u32[]{:S(2)}) async-start(bf16[1,4,768,384]{3,1,0,2:T(4,128)(2,1)} %copy.41), calls=%async_computation.3 | async-start | bytes 4718592 | tf_op jit(solution)/shard_map/all_to_all | solution.py:68
  283.1 1.4 copy-start.2
  284.5 33.2 %all-to-all-start.1 = ((bf16[1,4,768,384]{3,1,0,2:T(4,128)(2,1)}), bf16[1,4,768,384]{3,1,0,2:T(4,128)(2,1)}, u32[]{:S(2)}, u32[]{:S(2)}) async-start(bf16[1,4,768,384]{3,1,0,2:T(4,128)(2,1)} %copy.37), calls=%async_computation.1 | async-start | bytes 4718592 | tf_op jit(solution)/shard_map/all_to_all | solution.py:68
  289.1 2.6 copy-start.3
  328.8 5.0 %copy-start.4 = (f32[1024,384]{1,0:T(8,128)S(1)}, f32[1024,384]{1,0:T(8,128)}, u32[]{:S(2)}) copy-start(f32[1024,384]{1,0:T(8,128)} %convert_element_type.81) | copy-start | bytes 4718596
  328.8 5.0 %copy-start.5 = (f32[1024,2]{1,0:T(8,128)S(1)}, f32[1024,2]{1,0:T(8,128)}, u32[]{:S(2)}) copy-start(f32[1024,2]{1,0:T(8,128)} %copy.32) | copy-start | bytes 24580
Sparse Core Ops, SparseCore 0:
  10.2 62.7 all-gather.3
  75.2 58.6 all-gather.5
  136.1 58.6 all-gather.7
  220.1 73.3 reduce-scatter.3
  296.9 73.5 reduce-scatter.5
  374.0 73.5 reduce-scatter.7
where the time goes:
time: 463 us; the launch traced here: 456 us
  waiting for transfers between devices  228 us (49%)
  local copies, waits for them, and re-layouts  75.2 us (16%)
  matrix products  74.7 us (16%)
  other arithmetic  45.2 us (10%)
  starting transfers between devices  18.4 us (4%)
  between operations  14.6 us (3%)
    reduce_scatter x1, waiting for transfers between devices, on_device(): lax.psum_scatter(grad_down.astype(jnp.bfloat16), 'blk', scatter_dimension...  75 us
    all_gather x1, waiting for transfers between devices, on_device(): lax.all_gather(w_down, 'blk', axis=1, tiled=True)  52.6 us
    all_to_all x2, waiting for transfers between devices, to_experts(): lax.all_to_all(packed, 'tile', split_axis=0, concat_axis=2, tiled=True)[0]  31 us
    all_to_all x2, waiting for transfers between devices, from_experts(): lax.all_to_all(results[None], 'tile', split_axis=2, concat_axis=0, tiled=...  29.6 us
    all_gather x1, waiting for transfers between devices, on_device(): lax.all_gather(w_up, 'blk', axis=1, tiled=True)  22.5 us
    gather x2, local copies, waits for them, and re-layouts, from_experts(): picked = returned.reshape(experts_all * capacity, features)[slot_index]  18.1 us
    dot_general x1, matrix products, expert_backward(): jnp.einsum('erd,ehd->erh', d_rows, weight_down, preferred_element_type=jn...  18 us
    reduce_scatter x1, waiting for transfers between devices, on_device(): lax.psum_scatter(grad_up.astype(jnp.bfloat16), 'blk', scatter_dimension=1...  15.5 us
  transfers between devices with their start and end apart: 10, of which 8 were waited for; matrix products, arithmetic and copies ran while one was open for 36% of the time, Pallas kernels for 0%

commit v1 on v0

v1 whole, which is shorter than its diff:
```python
import functools
import math

import jax
import jax.numpy as jnp
from jax import lax
from jax.experimental import pallas as pl
from jax.experimental.pallas import tpu as pltpu
from jax.sharding import PartitionSpec as P

F32 = jnp.float32
BF16 = jnp.bfloat16
MESH = pl.DeviceIdType.MESH


def ring_order(count):
    inner = max(d for d in range(1, math.isqrt(count) + 1) if count % d == 0)
    outer = count // inner
    walk = [row * inner for row in range(outer)]
    for step, row in enumerate(reversed(range(outer))):
        cols = list(range(1, inner))
        if step % 2:
            cols.reverse()
        walk += [row * inner + col for col in cols]
    return walk


def lookup(table, index):
    total = jnp.int32(0)
    for place, value in enumerate(table):
        total = total + jnp.where(index == place, jnp.int32(value), jnp.int32(0))
    return total


def matmul(left, right, dims):
    return lax.dot_general(left, right, (dims, ((), ())), preferred_element_type=F32)


def kernel(
    tiles, blks, per_tile, cap,
    tok, gain, route, route_t, gates, w_gate, w_up, w_down, dmix,
    mixed, grad_gates, grad_tok, out_gu, out_dn,
    wgu, wdn, xs, ds, xr, dr, yr, dyr, ggu, gdn, rgu, rdn, tmp, slot_c, slot_r,
    load_sem, ag_send, ag_recv, rs_send, rs_recv, go_send, go_recv, go_own,
    back_send, back_recv, back_own,
):
    rows, feats = tok.shape
    hid = w_gate.shape[2]
    experts = tiles * per_tile
    half = hid // 2
    t = lax.axis_index("tile")
    b = lax.axis_index("blk")
    walk = ring_order(blks)
    where_is = [walk.index(i) for i in range(blks)]
    pos = lookup(where_is, b)

    def at(place):
        return lookup(walk, lax.rem(place + 4 * blks, blks))

    ring = (at(pos + 1), at(pos - 1))
    signs = (1, -1)

    def peer(jj):
        return lax.rem(t + jj, tiles)

    def source(jj):
        return lax.rem(t - jj + tiles, tiles)

    loads = []
    for index, (src, dst) in enumerate(
        ((w_gate, wgu.at[:, 0, b]), (w_up, wgu.at[:, 1, b]), (w_down, wdn.at[:, b]))
    ):
        loads.append(pltpu.make_async_copy(src, dst, load_sem.at[index]))
        loads[-1].start()

    barrier = pltpu.get_barrier_semaphore()
    for place in ring:
        pl.semaphore_signal(barrier, inc=1, device_id=(t, place), device_id_type=MESH)
    for jj in range(1, tiles):
        pl.semaphore_signal(barrier, inc=1, device_id=(peer(jj), b), device_id_type=MESH)
    pl.semaphore_wait(barrier, 2 + tiles - 1)
    for load in loads:
        load.wait()

    def ag_copies(e, s, way):
        owner = at(pos - signs[way] * s)
        return [
            pltpu.make_async_remote_copy(
                src_ref=ref, dst_ref=ref,
                send_sem=ag_send.at[e, way, s, part], recv_sem=ag_recv.at[e, way, s, part],
                device_id=(t, ring[way]), device_id_type=MESH,
            )
            for part, ref in enumerate((wgu.at[e, :, owner], wdn.at[e, owner]))
        ]

    def ag_wait_copies(e, s, way):
        owner = at(pos - signs[way] * (s + 1))
        return [
            pltpu.make_async_remote_copy(
                src_ref=ref, dst_ref=ref,
                send_sem=ag_send.at[e, way, s, part], recv_sem=ag_recv.at[e, way, s, part],
                device_id=(t, ring[way]), device_id_type=MESH,
            )
            for part, ref in enumerate((wgu.at[e, :, owner], wdn.at[e, owner]))
        ]

    hops = blks // 2

    def ag_each(e, s, action):
        for way in range(2):
            @pl.when(jnp.logical_or(s < hops - 1, jnp.logical_and(s == hops - 1, lax.rem(e, 2) == way)))
            def _():
                action(e, s, way)

    def ag_start(e, s):
        def go(e, s, way):
            for copy in ag_copies(e, s, way):
                copy.start()
        ag_each(e, s, go)

    def ag_wait(e, s):
        def land(e, s, way):
            for copy in ag_wait_copies(e, s, way):
                copy.wait_recv()
        ag_each(e, s, land)

    def ag_sent(e, s):
        def done(e, s, way):
            for copy in ag_copies(e, s, way):
                copy.wait_send()
        ag_each(e, s, done)

    def rs_copies(e, s, way):
        chunk = at(pos - signs[way] * (s + 1))
        return [
            pltpu.make_async_remote_copy(
                src_ref=src, dst_ref=dst,
                send_sem=rs_send.at[e, way, s, part], recv_sem=rs_recv.at[e, way, s, part],
                device_id=(t, ring[way]), device_id_type=MESH,
            )
            for part, (src, dst) in enumerate((
                (ggu.at[e, way, chunk], rgu.at[e, way, s]),
                (gdn.at[e, way, chunk], rdn.at[e, way, s]),
            ))
        ]

    def rs_start(e, s):
        for way in range(2):
            for copy in rs_copies(e, s, way):
                copy.start()

    last = blks - 2

    def rs_step(e, s):
        for way in range(2):
            for copy in rs_copies(e, s, way):
                copy.wait_recv()
            chunk = at(pos - signs[way] * (s + 2))
            gu = ggu[e, way, chunk].astype(F32) + rgu[e, way, s].astype(F32)
            dn = gdn[e, way, chunk].astype(F32) + rdn[e, way, s].astype(F32)

            @pl.when(s < last)
            def _():
                ggu[e, way, chunk] = gu.astype(BF16)
                gdn[e, way, chunk] = dn.astype(BF16)
                for copy in rs_copies(e, s + 1, way):
                    copy.start()

            @pl.when(s == last)
            def _():
                out_gu[e, way] = gu
                out_dn[e, way] = dn

    def row_copies(src, dst, send, recv, own, e, jj, part, place):
        def here():
            return pltpu.make_async_copy(src, dst, own.at[e, part])

        def there():
            return pltpu.make_async_remote_copy(
                src_ref=src, dst_ref=dst, send_sem=send.at[e, jj, part],
                recv_sem=recv.at[e, jj, part], device_id=(place, b), device_id_type=MESH,
            )

        return here, there

    def go_pairs(e, jj, at_tile):
        return [
            row_copies(src.at[e, jj], dst.at[e, at_tile], go_send, go_recv, go_own, e, jj, part, peer(jj))
            for part, (src, dst) in enumerate(((xs, xr), (ds, dr)))
        ]

    def back_pairs(e, jj, at_tile):
        return [
            row_copies(src.at[e, peer(jj)], dst.at[at_tile, e], back_send, back_recv, back_own, e, jj, part, peer(jj))
            for part, (src, dst) in enumerate(((xr, yr), (dr, dyr)))
        ]

    for e in range(min(2, per_tile)):
        ag_start(e, 0)

    block = min(256, rows)

    def slots(i, carry):
        base = pl.multiple_of(i * block, block)
        names = lax.broadcasted_iota(jnp.int32, (rows, experts), 1)
        count = (route[:, 0:1] == names).astype(F32) + (route[:, 1:2] == names).astype(F32)
        row = lax.broadcasted_iota(jnp.int32, (block, rows), 0) + base
        col = lax.broadcasted_iota(jnp.int32, (block, rows), 1)
        before = matmul((col < row).astype(F32).astype(BF16), count.astype(BF16), ((1,), (0,)))
        part = route[pl.ds(base, block), :]
        name = lax.broadcasted_iota(jnp.int32, (block, experts), 1)
        for k in range(2):
            mine = part[:, k : k + 1]
            rank = jnp.sum(jnp.where(mine == name, before, 0.0), axis=1, keepdims=True)
            slot_c[pl.ds(base, block), k : k + 1] = mine * cap + rank.astype(jnp.int32)
        names_t = lax.broadcasted_iota(jnp.int32, (experts, rows), 0)
        count_t = (route_t[0:1, :] == names_t).astype(F32) + (route_t[1:2, :] == names_t).astype(F32)
        row_t = lax.broadcasted_iota(jnp.int32, (rows, block), 0)
        col_t = lax.broadcasted_iota(jnp.int32, (rows, block), 1) + base
        before_t = matmul(count_t.astype(BF16), (row_t < col_t).astype(F32).astype(BF16), ((1,), (0,)))
        part_t = route_t[:, pl.ds(base, block)]
        name_t = lax.broadcasted_iota(jnp.int32, (experts, block), 0)
        for k in range(2):
            mine = part_t[k : k + 1, :]
            rank = jnp.sum(jnp.where(mine == name_t, before_t, 0.0), axis=0, keepdims=True)
            slot_r[k : k + 1, pl.ds(base, block)] = mine * cap + rank.astype(jnp.int32)
        x = tok[pl.ds(base, block), :].astype(F32)
        centred = x - jnp.mean(x, axis=-1, keepdims=True)
        spread = jnp.mean(centred * centred, axis=-1, keepdims=True)
        d = dmix[pl.ds(base, block), :].astype(F32)
        g = gates[pl.ds(base, block), :]
        tmp[0, pl.ds(base, block), 0:feats] = (x * lax.rsqrt(spread + 1e-05) * gain[...]).astype(BF16)
        tmp[1, pl.ds(base, block), 0:feats] = (g[:, 0:1] * d).astype(BF16)
        tmp[2, pl.ds(base, block), 0:feats] = (g[:, 1:2] * d).astype(BF16)
        return carry

    lax.fori_loop(0, rows // block, slots, 0)

    def pack(i, carry):
        e, jj = i // tiles, lax.rem(i, tiles)
        dest = peer(jj)
        want = lax.broadcasted_iota(jnp.int32, (cap, rows), 0) + (dest * per_tile + e) * cap
        first = (slot_r[0:1, :] == want).astype(F32)
        second = (slot_r[1:2, :] == want).astype(F32)
        xs[e, jj] = matmul((first + second).astype(BF16), tmp[0, 0:rows, 0:feats], ((1,), (0,))).astype(BF16)
        ds[e, jj] = (
            matmul(first.astype(BF16), tmp[1, 0:rows, 0:feats], ((1,), (0,)))
            + matmul(second.astype(BF16), tmp[2, 0:rows, 0:feats], ((1,), (0,)))
        ).astype(BF16)

        @pl.when(jj == 0)
        def _():
            for here, there in go_pairs(e, jj, t):
                here().start()

        @pl.when(jj > 0)
        def _():
            for here, there in go_pairs(e, jj, t):
                there().start()

        return carry

    lax.fori_loop(0, per_tile * tiles, pack, 0)

    for s in range(hops):
        for e in range(min(2, per_tile)):
            ag_wait(e, s)
            if s + 1 < hops:
                ag_start(e, s + 1)

    def service(e, k):
        @pl.when(jnp.logical_and(e + 2 < per_tile, k < hops))
        def _():
            ag_wait(e + 2, k)

            @pl.when(k + 1 < hops)
            def _():
                ag_start(e + 2, k + 1)

        @pl.when(jnp.logical_and(e >= 1, k <= last))
        def _():
            rs_step(e - 1, k)

    def expert(e, carry):
        @pl.when(e + 2 < per_tile)
        def _():
            ag_start(e + 2, 0)

        for jj in range(tiles):
            for here, there in go_pairs(e, jj, source(jj)):
                if jj == 0:
                    here().wait()
                else:
                    there().wait_recv()

        def forward(i, carry):
            span = pl.ds(pl.multiple_of(i * cap, cap), cap)
            x, d = xr[e, i], dr[e, i]
            wide = (feats, hid)
            gate_pre = matmul(x, wgu[e, 0].reshape(wide), ((1,), (0,)))
            up_pre = matmul(x, wgu[e, 1].reshape(wide), ((1,), (0,)))
            d_act = matmul(d, wdn[e].reshape(hid, feats), ((1,), (1,)))
            sigma = jax.nn.sigmoid(gate_pre)
            swish = gate_pre * sigma
            tmp[0, span, :] = (swish * up_pre).astype(BF16)
            tmp[1, span, :] = (d_act * up_pre * sigma * (1.0 + gate_pre * (1.0 - sigma))).astype(BF16)
            tmp[2, span, :] = (d_act * swish).astype(BF16)
            service(e, i)
            return carry

        lax.fori_loop(0, tiles, forward, 0)

        many = tiles * cap
        x_all = xr[e].reshape(many, feats)
        for part in range(2):
            for way in range(2):
                grad = matmul(x_all, tmp[1 + part, 0:many, way * half : (way + 1) * half], ((0,), (0,)))
                ggu[e, way, :, part] = grad.reshape(blks, feats // blks, half).astype(BF16)
        width = min(256, hid)
        deep = hid // blks

        def down(i, carry):
            span = pl.ds(pl.multiple_of(i * width, width), width)
            grad = matmul(tmp[0, 0:many, span], dr[e].reshape(many, feats), ((0,), (0,)))
            grad = grad.reshape(width // deep, 2, deep // 2, feats).astype(BF16)
            for c in range(width // deep):
                for way in range(2):
                    gdn[e, way, i * (width // deep) + c] = grad[c, way]
            return carry

        lax.fori_loop(0, hid // width, down, 0)
        rs_start(e, 0)

        def backward(i, carry):
            span = pl.ds(pl.multiple_of(i * cap, cap), cap)
            wide = (feats, hid)
            y = matmul(tmp[0, span, :], wdn[e].reshape(hid, feats), ((1,), (0,)))
            d_in = matmul(tmp[1, span, :], wgu[e, 0].reshape(wide), ((1,), (1,)))
            d_in = d_in + matmul(tmp[2, span, :], wgu[e, 1].reshape(wide), ((1,), (1,)))
            xr[e, i] = y.astype(BF16)
            dr[e, i] = d_in.astype(BF16)
            service(e, tiles + i)
            return carry

        lax.fori_loop(0, tiles, backward, 0)
        for jj in range(tiles):
            for here, there in back_pairs(e, jj, t):
                (there if jj else here)().start()

        def rest(i, carry):
            service(e, i)
            return carry

        lax.fori_loop(2 * tiles, max(2 * tiles, blks - 1, hops), rest, 0)
        return carry

    lax.fori_loop(0, per_tile, expert, 0)

    def returned(e, carry):
        for jj in range(tiles):
            for here, there in back_pairs(e, jj, source(jj)):
                if jj == 0:
                    here().wait()
                else:
                    there().wait_recv()
        return carry

    lax.fori_loop(0, per_tile, returned, 0)

    def finish(i):
        base = pl.multiple_of(i * block, block)
        span = pl.ds(base, block)
        every = experts * cap
        want = lax.broadcasted_iota(jnp.int32, (block, every), 1)
        first = (slot_c[span, 0:1] == want).astype(F32)
        second = (slot_c[span, 1:2] == want).astype(F32)
        y = yr[...].reshape(every, feats)
        y0 = matmul(first.astype(BF16), y, ((1,), (0,)))
        y1 = matmul(second.astype(BF16), y, ((1,), (0,)))
        dn = matmul((first + second).astype(BF16), dyr[...].reshape(every, feats), ((1,), (0,)))
        g = gates[span, :]
        d = dmix[span, :].astype(F32)
        mixed[span, :] = (g[:, 0:1] * y0 + g[:, 1:2] * y1).astype(BF16)
        grad_gates[span, 0:1] = jnp.sum(d * y0, axis=-1, keepdims=True)
        grad_gates[span, 1:2] = jnp.sum(d * y1, axis=-1, keepdims=True)
        x = tok[span, :].astype(F32)
        centred = x - jnp.mean(x, axis=-1, keepdims=True)
        spread = jnp.mean(centred * centred, axis=-1, keepdims=True)
        r = lax.rsqrt(spread + 1e-05)
        u = dn * gain[...]
        pull = jnp.sum(u * x, axis=-1, keepdims=True) * (r * r * r) / feats
        grad_tok[span, :] = (u * r - pull * centred).astype(BF16)

    def tail(s, carry):
        @pl.when(s <= last)
        def _():
            rs_step(per_tile - 1, s)

        @pl.when(s < rows // block)
        def _():
            finish(s)

        return carry

    lax.fori_loop(0, max(blks - 1, rows // block), tail, 0)

    def drain(e, carry):
        def ag_done(s, carry):
            ag_sent(e, s)
            return carry

        lax.fori_loop(0, hops, ag_done, 0)

        def rs_done(s, carry):
            for way in range(2):
                for copy in rs_copies(e, s, way):
                    copy.wait_send()
            return carry

        lax.fori_loop(0, blks - 1, rs_done, 0)
        for jj in range(1, tiles):
            for here, there in go_pairs(e, jj, t) + back_pairs(e, jj, t):
                there().wait_send()
        return carry

    lax.fori_loop(0, per_tile, drain, 0)


def on_device(tiles, blks, tokens, ln_gain, route, gates, w_gate, w_up, w_down, d_mixed):
    rows, feats = tokens.shape
    per_tile, thin, hid = w_gate.shape
    deep = w_down.shape[1]
    experts = per_tile * tiles
    cap = max(2, 3 * rows * route.shape[1] // (2 * experts))
    half = hid // 2
    hops = blks // 2
    vmem = pl.BlockSpec(memory_space=pltpu.VMEM)
    hbm = pl.BlockSpec(memory_space=pl.ANY)
    moved = (per_tile, tiles, cap, feats)
    dma = pltpu.SemaphoreType.DMA
    outs = pl.pallas_call(
        functools.partial(kernel, tiles, blks, per_tile, cap),
        out_shape=(
            jax.ShapeDtypeStruct((rows, feats), BF16),
            jax.ShapeDtypeStruct((rows, 2), F32),
            jax.ShapeDtypeStruct((rows, feats), BF16),
            jax.ShapeDtypeStruct((per_tile, 2, 2, thin, half), F32),
            jax.ShapeDtypeStruct((per_tile, 2, deep // 2, feats), F32),
        ),
        in_specs=[vmem, vmem, vmem, vmem, vmem, hbm, hbm, hbm, vmem],
        out_specs=[vmem] * 5,
        scratch_shapes=[
            pltpu.VMEM((per_tile, 2, blks, thin, hid), BF16),
            pltpu.VMEM((per_tile, blks, deep, feats), BF16),
            pltpu.VMEM(moved, BF16),
            pltpu.VMEM(moved, BF16),
            pltpu.VMEM(moved, BF16),
            pltpu.VMEM(moved, BF16),
            pltpu.VMEM((tiles, per_tile, cap, feats), BF16),
            pltpu.VMEM((tiles, per_tile, cap, feats), BF16),
            pltpu.VMEM((per_tile, 2, blks, 2, thin, half), BF16),
            pltpu.VMEM((per_tile, 2, blks, deep // 2, feats), BF16),
            pltpu.VMEM((per_tile, 2, blks - 1, 2, thin, half), BF16),
            pltpu.VMEM((per_tile, 2, blks - 1, deep // 2, feats), BF16),
            pltpu.VMEM((3, max(rows, tiles * cap), max(hid, feats)), BF16),
            pltpu.VMEM((rows, 2), jnp.int32),
            pltpu.VMEM((2, rows), jnp.int32),
            dma((3,)),
            dma((per_tile, 2, hops, 2)),
            dma((per_tile, 2, hops, 2)),
            dma((per_tile, 2, blks - 1, 2)),
            dma((per_tile, 2, blks - 1, 2)),
            dma((per_tile, tiles, 2)),
            dma((per_tile, tiles, 2)),
            dma((per_tile, 2)),
            dma((per_tile, tiles, 2)),
            dma((per_tile, tiles, 2)),
            dma((per_tile, 2)),
        ],
        compiler_params=pltpu.CompilerParams(
            collective_id=0, has_side_effects=True, vmem_limit_bytes=67043328
        ),
    )(tokens, ln_gain.reshape(1, feats), route, route.T, gates, w_gate, w_up, w_down, d_mixed)
    mixed, grad_gates, grad_tokens, gu, dn = outs
    gu = gu.transpose(2, 0, 3, 1, 4).reshape(2, per_tile, thin, hid)
    return (mixed, grad_gates, grad_tokens, gu[0], gu[1], dn.reshape(per_tile, deep, feats))


def solution(mesh):
    rows_spec = P(("tile", "blk"), None)
    weight_spec = P("tile", "blk", None)
    return jax.shard_map(
        functools.partial(on_device, mesh.shape["tile"], mesh.shape["blk"]),
        mesh=mesh,
        in_specs=(rows_spec, P(), rows_spec, rows_spec) + (weight_spec,) * 3 + (rows_spec,),
        out_specs=(rows_spec,) * 3 + (weight_spec,) * 3,
        check_vma=False,
    )
```

time: 463 us -> 274 us (0.59); the launches traced: 456 us -> 274 us
  Pallas kernels: 0 us -> 258 us
  waiting for transfers between devices: 228 us -> 0 us
  matrix products: 74.7 us -> 0 us
  local copies, waits for them, and re-layouts: 75.2 us -> 15 us
  other arithmetic: 45.2 us -> 0 us
  starting transfers between devices: 18.4 us -> 0 us
  between operations: 14.6 us -> 0.67 us
    pallas_call x0 -> x1, Pallas kernels: none -> 258 us  [on_device(): pl.pallas_call(functools.partial(kernel, tiles, blks, per_tile, cap), out...]
    reduce_scatter x3 -> x0, waiting for transfers between devices: 90.6 us -> none  [the longest x1 75 us: on_device(): lax.psum_scatter(grad_down.astype(jnp.bfloat16), 'blk', scatter_dimension...]
    all_gather x3 -> x0, waiting for transfers between devices: 75 us -> none  [the longest x1 52.6 us: on_device(): lax.all_gather(w_down, 'blk', axis=1, tiled=True)]
    dot_general x9 -> x0, matrix products: 74.7 us -> none  [the longest x1 18 us: expert_backward(): jnp.einsum('erd,ehd->erh', d_rows, weight_down, preferred_element_type=jn...]
    all_to_all x4 -> x0, waiting for transfers between devices: 60.6 us -> none  [the longest x2 31 us: to_experts(): lax.all_to_all(packed, 'tile', split_axis=0, concat_axis=2, tiled=True)[0]]
    gather x2 -> x0, local copies, waits for them, and re-layouts: 18.1 us -> none  [from_experts(): picked = returned.reshape(experts_all * capacity, features)[slot_index]]
    all_to_all x4 -> x0, starting transfers between devices: 17.6 us -> none  [the longest x2 9.31 us: to_experts(): lax.all_to_all(packed, 'tile', split_axis=0, concat_axis=2, tiled=True)[0]]
    reduce_sum x7 -> x0, other arithmetic: 17.2 us -> none  [the longest x1 10.1 us: on_device(): grad_gates = jnp.sum(d_wide[:, None, :] * expert_out, axis=-1)]
  transfers between devices with their start and end apart: 10 -> 0, of which waited for: 8 -> 0; matrix products, arithmetic and copies ran while one was open for 36% -> 0% of each run, Pallas kernels for 0% -> 0%
where the time goes in v1:
time: 274 us
  Pallas kernels  258 us (94%)
  local copies, waits for them, and re-layouts  15 us (5%)
    pallas_call x1, Pallas kernels, on_device(): pl.pallas_call(functools.partial(kernel, tiles, blks, per_tile, cap), out...  258 us
    unnamed x12, local copies, waits for them, and re-layouts  7.91 us

profile of v1, /device:TPU:0, one launch (start us, length us, event | category | flops | bytes accessed | tf_op | source)
XLA Modules:
  0.0 273.5 jit_solution(5513543624617198420)
XLA Ops:
  0.6 1.2 reshape.23.gain
  1.9 1.7 copy.18.gates
  3.6 1.7 copy.17.route
  5.3 257.8 %shard_map.127 = (bf16[1024,384]{1,0:T(8,128)(2,1)}, f32[1024,2]{1,0:T(8,128)}, bf16[1024,384]{1,0:T(8,128)(2,1)}, f32[4,2,2,48,512]{4,3,2,1,0:T(8,128)}, f32[4,2,64,384]{3,2,1,0:T(8,128)}) custom-call(bf16[1024,384]{1,0:T(8,128)(2,1)} %tok.1, f32[1,384]{1,0:T(1,128)} %reshape.23.gain, s32[1024,2]{1,0:T(8,128)} %copy.17.route, s32[2,1024]{1,0:T(2,128)} %bitcast.5, ...), custom_call_target="tpu_custom_call" | custom-call | tf_op jit(solution)/shard_map/pallas_call | solution.py:441
  263.1 1.8 copy.21
  265.0 1.5 fusion
  266.5 0.6 copy.20
  267.1 1.6 squeeze.7
  268.7 0.0 copy-start.2
  268.7 0.6 copy.19
  269.3 0.0 copy-start.1
  269.3 1.6 squeeze.6
  270.9 0.0 copy-done.2
  270.9 0.0 copy-start
  270.9 0.9 copy.25
  271.7 0.0 copy-done.1
  271.7 0.9 copy.26
  272.6 0.0 copy-done
  272.6 0.9 copy.27
Async XLA Ops:
  268.7 2.2 copy-start.2
  269.3 2.5 copy-start.1
  270.9 1.8 copy-start

commit v2 on v1

--- a/solution.py
+++ b/solution.py
@@ -36,11 +36,19 @@
     return lax.dot_general(left, right, (dims, ((), ())), preferred_element_type=F32)
 
 
+class Later:
+    def __init__(self, **parts):
+        self.parts = parts
+
+    def __getattr__(self, name):
+        return getattr(pltpu.make_async_remote_copy(**self.parts), name)
+
+
 def kernel(
     tiles, blks, per_tile, cap,
-    tok, gain, route, route_t, gates, w_gate, w_up, w_down, dmix,
-    mixed, grad_gates, grad_tok, out_gu, out_dn,
-    wgu, wdn, xs, ds, xr, dr, yr, dyr, ggu, gdn, rgu, rdn, tmp, slot_c, slot_r,
+    tok, gain, route_t, gates_t, w_gate, w_up, w_down, dmix,
+    mixed, grad_gates, grad_tok, out_gate, out_up, out_dn,
+    wgu, wdn, xs, ds, xr, dr, yr, dyr, ggu, gdn, rgu, rdn, tmp, cols, slot_r,
     load_sem, ag_send, ag_recv, rs_send, rs_recv, go_send, go_recv, go_own,
     back_send, back_recv, back_own,
 ):
@@ -48,6 +56,7 @@
     hid = w_gate.shape[2]
     experts = tiles * per_tile
     half = hid // 2
+    deep = hid // blks
     t = lax.axis_index("tile")
     b = lax.axis_index("blk")
     walk = ring_order(blks)
@@ -133,7 +142,7 @@
     def rs_copies(e, s, way):
         chunk = at(pos - signs[way] * (s + 1))
         return [
-            pltpu.make_async_remote_copy(
+            Later(
                 src_ref=src, dst_ref=dst,
                 send_sem=rs_send.at[e, way, s, part], recv_sem=rs_recv.at[e, way, s, part],
                 device_id=(t, ring[way]), device_id_type=MESH,
@@ -152,24 +161,24 @@
     last = blks - 2
 
     def rs_step(e, s):
-        for way in range(2):
-            for copy in rs_copies(e, s, way):
-                copy.wait_recv()
-            chunk = at(pos - signs[way] * (s + 2))
-            gu = ggu[e, way, chunk].astype(F32) + rgu[e, way, s].astype(F32)
-            dn = gdn[e, way, chunk].astype(F32) + rdn[e, way, s].astype(F32)
-
-            @pl.when(s < last)
-            def _():
-                ggu[e, way, chunk] = gu.astype(BF16)
-                gdn[e, way, chunk] = dn.astype(BF16)
-                for copy in rs_copies(e, s + 1, way):
-                    copy.start()
-
-            @pl.when(s == last)
-            def _():
-                out_gu[e, way] = gu
-                out_dn[e, way] = dn
+        for part, (own, landed) in enumerate(((ggu, rgu), (gdn, rdn))):
+            for way in range(2):
+                rs_copies(e, s, way)[part].wait_recv()
+                chunk = at(pos - signs[way] * (s + 2))
+                total = own[e, way, chunk].astype(F32) + landed[e, way, s].astype(F32)
+
+                @pl.when(s < last)
+                def _():
+                    own[e, way, chunk] = total.astype(BF16)
+                    rs_copies(e, s + 1, way)[part].start()
+
+                @pl.when(s == last)
+                def _():
+                    if part:
+                        out_dn[e, way * (deep // 2) : (way + 1) * (deep // 2), :] = total
+                    else:
+                        out_gate[e, :, way * half : (way + 1) * half] = total[0]
+                        out_up[e, :, way * half : (way + 1) * half] = total[1]
 
     def row_copies(src, dst, send, recv, own, e, jj, part, place):
         def here():
@@ -202,36 +211,32 @@
 
     def slots(i, carry):
         base = pl.multiple_of(i * block, block)
-        names = lax.broadcasted_iota(jnp.int32, (rows, experts), 1)
-        count = (route[:, 0:1] == names).astype(F32) + (route[:, 1:2] == names).astype(F32)
-        row = lax.broadcasted_iota(jnp.int32, (block, rows), 0) + base
-        col = lax.broadcasted_iota(jnp.int32, (block, rows), 1)
-        before = matmul((col < row).astype(F32).astype(BF16), count.astype(BF16), ((1,), (0,)))
-        part = route[pl.ds(base, block), :]
-        name = lax.broadcasted_iota(jnp.int32, (block, experts), 1)
+        span = pl.ds(base, block)
+        names = lax.broadcasted_iota(jnp.int32, (experts, rows), 0)
+        count = (route_t[0:1, :] == names).astype(F32) + (route_t[1:2, :] == names).astype(F32)
+        row = lax.broadcasted_iota(jnp.int32, (rows, block), 0)
+        col = lax.broadcasted_iota(jnp.int32, (rows, block), 1) + base
+        before = matmul(count.astype(BF16), (row < col).astype(F32).astype(BF16), ((1,), (0,)))
+        part = route_t[:, span]
+        name = lax.broadcasted_iota(jnp.int32, (experts, block), 0)
+        line = lax.broadcasted_iota(jnp.int32, (8, block), 0)
+        stack = jnp.zeros((8, block), F32)
         for k in range(2):
-            mine = part[:, k : k + 1]
-            rank = jnp.sum(jnp.where(mine == name, before, 0.0), axis=1, keepdims=True)
-            slot_c[pl.ds(base, block), k : k + 1] = mine * cap + rank.astype(jnp.int32)
-        names_t = lax.broadcasted_iota(jnp.int32, (experts, rows), 0)
-        count_t = (route_t[0:1, :] == names_t).astype(F32) + (route_t[1:2, :] == names_t).astype(F32)
-        row_t = lax.broadcasted_iota(jnp.int32, (rows, block), 0)
-        col_t = lax.broadcasted_iota(jnp.int32, (rows, block), 1) + base
-        before_t = matmul(count_t.astype(BF16), (row_t < col_t).astype(F32).astype(BF16), ((1,), (0,)))
-        part_t = route_t[:, pl.ds(base, block)]
-        name_t = lax.broadcasted_iota(jnp.int32, (experts, block), 0)
-        for k in range(2):
-            mine = part_t[k : k + 1, :]
-            rank = jnp.sum(jnp.where(mine == name_t, before_t, 0.0), axis=0, keepdims=True)
-            slot_r[k : k + 1, pl.ds(base, block)] = mine * cap + rank.astype(jnp.int32)
-        x = tok[pl.ds(base, block), :].astype(F32)
+            mine = part[k : k + 1, :]
+            rank = jnp.sum(jnp.where(mine == name, before, 0.0), axis=0, keepdims=True)
+            slot = mine * cap + rank.astype(jnp.int32)
+            slot_r[k : k + 1, span] = slot
+            stack = jnp.where(line == k, slot.astype(F32), stack)
+            stack = jnp.where(line == k + 2, gates_t[k : k + 1, span], stack)
+        turned = stack.T
+        cols[span, :] = turned
+        x = tok[span, :].astype(F32)
         centred = x - jnp.mean(x, axis=-1, keepdims=True)
         spread = jnp.mean(centred * centred, axis=-1, keepdims=True)
-        d = dmix[pl.ds(base, block), :].astype(F32)
-        g = gates[pl.ds(base, block), :]
-        tmp[0, pl.ds(base, block), 0:feats] = (x * lax.rsqrt(spread + 1e-05) * gain[...]).astype(BF16)
-        tmp[1, pl.ds(base, block), 0:feats] = (g[:, 0:1] * d).astype(BF16)
-        tmp[2, pl.ds(base, block), 0:feats] = (g[:, 1:2] * d).astype(BF16)
+        d = dmix[span, :].astype(F32)
+        tmp[0, span, 0:feats] = (x * lax.rsqrt(spread + 1e-05) * gain[...]).astype(BF16)
+        tmp[1, span, 0:feats] = (turned[:, 2:3] * d).astype(BF16)
+        tmp[2, span, 0:feats] = (turned[:, 3:4] * d).astype(BF16)
         return carry
 
     lax.fori_loop(0, rows // block, slots, 0)
@@ -258,34 +263,56 @@
             for here, there in go_pairs(e, jj, t):
                 there().start()
 
-        return carry
+        @pl.when(jnp.logical_and(lax.rem(i, 4) == 3, i // 4 < hops))
+        def _():
+            ag_event(2 * (i // 4))
+            ag_event(2 * (i // 4) + 1)
+
+        return carry
+
+    def ag_event(j):
+        e = 2 * (j // (2 * hops)) + lax.rem(j, 2)
+        s = lax.rem(j // 2, hops)
+        ag_wait(e, s)
+
+        @pl.when(s + 1 < hops)
+        def _():
+            ag_start(e, s + 1)
+
+        @pl.when(jnp.logical_and(s == hops - 1, e + 2 < per_tile))
+        def _():
+            ag_start(e + 2, 0)
 
     lax.fori_loop(0, per_tile * tiles, pack, 0)
 
-    for s in range(hops):
-        for e in range(min(2, per_tile)):
-            ag_wait(e, s)
-            if s + 1 < hops:
-                ag_start(e, s + 1)
+    def late(j, carry):
+        ag_event(j)
+        return carry
+
+    lax.fori_loop(min(2 * hops, 2 * (per_tile * tiles // 4)), 2 * hops, late, 0)
+    points = 2 * tiles
+
+    def service_rs(e, k):
+        old, young = points // 2 + k // 2, k // 2
+
+        @pl.when(jnp.logical_and(jnp.logical_and(e >= 2, e - 2 < per_tile), jnp.logical_and(lax.rem(k, 2) == 0, old <= last)))
+        def _():
+            rs_step(e - 2, old)
+
+        @pl.when(jnp.logical_and(jnp.logical_and(e >= 1, e - 1 < per_tile), jnp.logical_and(lax.rem(k, 2) == 1, young <= last)))
+        def _():
+            rs_step(e - 1, young)
 
     def service(e, k):
-        @pl.when(jnp.logical_and(e + 2 < per_tile, k < hops))
-        def _():
-            ag_wait(e + 2, k)
-
-            @pl.when(k + 1 < hops)
-            def _():
-                ag_start(e + 2, k + 1)
-
-        @pl.when(jnp.logical_and(e >= 1, k <= last))
-        def _():
-            rs_step(e - 1, k)
+        j = 2 * hops + (e * points + k) // 2
+
+        @pl.when(jnp.logical_and(lax.rem(k, 2) == 0, j < per_tile * hops))
+        def _():
+            ag_event(j)
+
+        service_rs(e, k)
 
     def expert(e, carry):
-        @pl.when(e + 2 < per_tile)
-        def _():
-            ag_start(e + 2, 0)
-
         for jj in range(tiles):
             for here, there in go_pairs(e, jj, source(jj)):
                 if jj == 0:
@@ -317,7 +344,6 @@
                 grad = matmul(x_all, tmp[1 + part, 0:many, way * half : (way + 1) * half], ((0,), (0,)))
                 ggu[e, way, :, part] = grad.reshape(blks, feats // blks, half).astype(BF16)
         width = min(256, hid)
-        deep = hid // blks
 
         def down(i, carry):
             span = pl.ds(pl.multiple_of(i * width, width), width)
@@ -331,7 +357,9 @@
         lax.fori_loop(0, hid // width, down, 0)
         rs_start(e, 0)
 
-        def backward(i, carry):
+        def backward(ii, carry):
+            jj = lax.rem(ii + 1, tiles)
+            i = peer(jj)
             span = pl.ds(pl.multiple_of(i * cap, cap), cap)
             wide = (feats, hid)
             y = matmul(tmp[0, span, :], wdn[e].reshape(hid, feats), ((1,), (0,)))
@@ -339,19 +367,21 @@
             d_in = d_in + matmul(tmp[2, span, :], wgu[e, 1].reshape(wide), ((1,), (1,)))
             xr[e, i] = y.astype(BF16)
             dr[e, i] = d_in.astype(BF16)
-            service(e, tiles + i)
+            service(e, tiles + ii)
+
+            @pl.when(jj == 0)
+            def _():
+                for here, there in back_pairs(e, jj, t):
+                    here().start()
+
+            @pl.when(jj > 0)
+            def _():
+                for here, there in back_pairs(e, jj, t):
+                    there().start()
+
             return carry
 
         lax.fori_loop(0, tiles, backward, 0)
-        for jj in range(tiles):
-            for here, there in back_pairs(e, jj, t):
-                (there if jj else here)().start()
-
-        def rest(i, carry):
-            service(e, i)
-            return carry
-
-        lax.fori_loop(2 * tiles, max(2 * tiles, blks - 1, hops), rest, 0)
         return carry
 
     lax.fori_loop(0, per_tile, expert, 0)
@@ -365,24 +395,26 @@
                     there().wait_recv()
         return carry
 
-    lax.fori_loop(0, per_tile, returned, 0)
+    few = min(128, rows)
 
     def finish(i):
-        base = pl.multiple_of(i * block, block)
-        span = pl.ds(base, block)
+        base = pl.multiple_of(i * few, few)
+        span = pl.ds(base, few)
+        column = cols[span, :]
         every = experts * cap
-        want = lax.broadcasted_iota(jnp.int32, (block, every), 1)
-        first = (slot_c[span, 0:1] == want).astype(F32)
-        second = (slot_c[span, 1:2] == want).astype(F32)
+        want = lax.broadcasted_iota(jnp.int32, (few, every), 1)
+        first = (column[:, 0:1].astype(jnp.int32) == want).astype(F32)
+        second = (column[:, 1:2].astype(jnp.int32) == want).astype(F32)
         y = yr[...].reshape(every, feats)
         y0 = matmul(first.astype(BF16), y, ((1,), (0,)))
         y1 = matmul(second.astype(BF16), y, ((1,), (0,)))
         dn = matmul((first + second).astype(BF16), dyr[...].reshape(every, feats), ((1,), (0,)))
-        g = gates[span, :]
         d = dmix[span, :].astype(F32)
-        mixed[span, :] = (g[:, 0:1] * y0 + g[:, 1:2] * y1).astype(BF16)
-        grad_gates[span, 0:1] = jnp.sum(d * y0, axis=-1, keepdims=True)
-        grad_gates[span, 1:2] = jnp.sum(d * y1, axis=-1, keepdims=True)
+        mixed[span, :] = (column[:, 2:3] * y0 + column[:, 3:4] * y1).astype(BF16)
+        lane = lax.broadcasted_iota(jnp.int32, (few, 128), 1)
+        dots = jnp.where(lane == 0, jnp.sum(d * y0, axis=-1, keepdims=True), 0.0)
+        dots = jnp.where(lane == 1, jnp.sum(d * y1, axis=-1, keepdims=True), dots)
+        grad_gates[:, span] = dots.T[0:2, :]
         x = tok[span, :].astype(F32)
         centred = x - jnp.mean(x, axis=-1, keepdims=True)
         spread = jnp.mean(centred * centred, axis=-1, keepdims=True)
@@ -391,18 +423,22 @@
         pull = jnp.sum(u * x, axis=-1, keepdims=True) * (r * r * r) / feats
         grad_tok[span, :] = (u * r - pull * centred).astype(BF16)
 
-    def tail(s, carry):
-        @pl.when(s <= last)
-        def _():
-            rs_step(per_tile - 1, s)
-
-        @pl.when(s < rows // block)
-        def _():
-            finish(s)
-
-        return carry
-
-    lax.fori_loop(0, max(blks - 1, rows // block), tail, 0)
+    begin = points // 2
+
+    def tail(k, carry):
+        service_rs(per_tile + k // points, lax.rem(k, points))
+
+        @pl.when(k == begin)
+        def _():
+            lax.fori_loop(0, per_tile, returned, 0)
+
+        @pl.when(jnp.logical_and(k >= begin, k < begin + rows // few))
+        def _():
+            finish(k - begin)
+
+        return carry
+
+    lax.fori_loop(0, max(2 * points, begin + rows // few), tail, 0)
 
     def drain(e, carry):
         def ag_done(s, carry):
@@ -442,13 +478,14 @@
         functools.partial(kernel, tiles, blks, per_tile, cap),
         out_shape=(
             jax.ShapeDtypeStruct((rows, feats), BF16),
-            jax.ShapeDtypeStruct((rows, 2), F32),
+            jax.ShapeDtypeStruct((2, rows), F32),
             jax.ShapeDtypeStruct((rows, feats), BF16),
-            jax.ShapeDtypeStruct((per_tile, 2, 2, thin, half), F32),
-            jax.ShapeDtypeStruct((per_tile, 2, deep // 2, feats), F32),
+            jax.ShapeDtypeStruct((per_tile, thin, hid), F32),
+            jax.ShapeDtypeStruct((per_tile, thin, hid), F32),
+            jax.ShapeDtypeStruct((per_tile, deep, feats), F32),
         ),
-        in_specs=[vmem, vmem, vmem, vmem, vmem, hbm, hbm, hbm, vmem],
-        out_specs=[vmem] * 5,
+        in_specs=[vmem, vmem, vmem, vmem, hbm, hbm, hbm, vmem],
+        out_specs=[vmem] * 6,
         scratch_shapes=[
             pltpu.VMEM((per_tile, 2, blks, thin, hid), BF16),
             pltpu.VMEM((per_tile, blks, deep, feats), BF16),
@@ -463,7 +500,7 @@
             pltpu.VMEM((per_tile, 2, blks - 1, 2, thin, half), BF16),
             pltpu.VMEM((per_tile, 2, blks - 1, deep // 2, feats), BF16),
             pltpu.VMEM((3, max(rows, tiles * cap), max(hid, feats)), BF16),
-            pltpu.VMEM((rows, 2), jnp.int32),
+            pltpu.VMEM((rows, 8), F32),
             pltpu.VMEM((2, rows), jnp.int32),
             dma((3,)),
             dma((per_tile, 2, hops, 2)),
@@ -480,10 +517,8 @@
         compiler_params=pltpu.CompilerParams(
             collective_id=0, has_side_effects=True, vmem_limit_bytes=67043328
         ),
-    )(tokens, ln_gain.reshape(1, feats), route, route.T, gates, w_gate, w_up, w_down, d_mixed)
-    mixed, grad_gates, grad_tokens, gu, dn = outs
-    gu = gu.transpose(2, 0, 3, 1, 4).reshape(2, per_tile, thin, hid)
-    return (mixed, grad_gates, grad_tokens, gu[0], gu[1], dn.reshape(per_tile, deep, feats))
+    )(tokens, ln_gain.reshape(1, feats), route.T, gates.T, w_gate, w_up, w_down, d_mixed)
+    return (outs[0], outs[1].T) + tuple(outs[2:])
 
 
 def solution(mesh):

time: 274 us -> 215 us (0.78)
  Pallas kernels: 258 us -> 204 us
  local copies, waits for them, and re-layouts: 15 us -> 9.14 us
    pallas_call x1, Pallas kernels: 258 us -> 204 us  [on_device(): pl.pallas_call(functools.partial(kernel, tiles, blks, per_tile, cap), out...]
    squeeze x2 -> x0, local copies, waits for them, and re-layouts: 3.11 us -> none  [the longest x1 1.55 us: on_device(): gu[1]]
    slice x3 -> x0, local copies, waits for them, and re-layouts: 2.76 us -> none  [the longest x2 2.16 us: on_device(): gu[1]]
    unnamed x12 -> x18, local copies, waits for them, and re-layouts: 7.91 us -> 8.57 us
where the time goes in v2:
time: 215 us; the launch traced here: 214 us
  Pallas kernels  204 us (95%)
  local copies, waits for them, and re-layouts  9.14 us (4%)
    pallas_call x1, Pallas kernels, on_device(): pl.pallas_call(functools.partial(kernel, tiles, blks, per_tile, cap), out...  204 us
    unnamed x18, local copies, waits for them, and re-layouts  8.57 us

profile of v2, /device:TPU:0, one launch (start us, length us, event | category | flops | bytes accessed | tf_op | source)
XLA Modules:
  0.0 214.3 jit_solution(2443851505164798478)
XLA Ops:
  0.6 0.0 copy-start.5
  0.6 0.7 copy-done.5
  1.3 0.6 reshape.15.gain
  1.9 204.5 %shard_map.127 = (bf16[1024,384]{1,0:T(8,128)(2,1)}, f32[2,1024]{1,0:T(2,128)}, bf16[1024,384]{1,0:T(8,128)(2,1)}, f32[4,48,1024]{2,1,0:T(8,128)}, f32[4,48,1024]{2,1,0:T(8,128)}, /*index=5*/f32[4,128,384]{2,1,0:T(8,128)}) custom-call(bf16[1024,384]{1,0:T(8,128)(2,1)} %tok.1, f32[1,384]{1,0:T(1,128)} %reshape.15.gain, s32[2,1024]{1,0:T(2,128)} %bitcast.3, ...), custom_call_target="tpu_custom_call" | custom-call | tf_op jit(solution)/shard_map/pallas_call | solution.py:477
  206.4 0.0 copy-start.4
  206.4 0.0 copy-start.3
  206.4 2.2 %copy.20 = bf16[1024,384]{1,0:T(8,128)(2,1)} copy(bf16[1024,384]{1,0:T(8,128)(2,1)} %get-tuple-element.24) | data formatting | bytes 1572864
  208.5 0.0 copy-done.4
  208.5 0.6 copy.21
  209.1 0.0 copy-done.3
  209.1 0.0 copy-start.2
  209.2 0.9 copy.22
  210.0 0.5 copy-done.2
  210.6 0.0 copy-start.1
  210.6 0.9 copy.23
  211.4 0.5 copy-done.1
  212.0 0.0 copy-start
  212.0 0.9 copy.24
  212.9 0.5 copy-done
  213.4 0.9 copy.25
Async XLA Ops:
  0.6 0.7 copy-start.5
  206.4 2.2 %copy-start.4 = (f32[2,1024]{1,0:T(2,128)S(1)}, f32[2,1024]{1,0:T(2,128)}, u32[]{:S(2)}) copy-start(f32[2,1024]{1,0:T(2,128)} %get-tuple-element.13) | copy-start | bytes 24580
  206.4 2.8 %copy-start.3 = (bf16[1024,384]{1,0:T(8,128)(2,1)S(1)}, bf16[1024,384]{1,0:T(8,128)(2,1)}, u32[]{:S(2)}) copy-start(bf16[1024,384]{1,0:T(8,128)(2,1)} %get-tuple-element.26) | copy-start | bytes 2359300
  209.1 1.4 copy-start.2
  210.6 1.4 copy-start.1
  212.0 1.4 copy-start

commit v3 on v2

--- a/solution.py
+++ b/solution.py
@@ -204,7 +204,7 @@
             for part, (src, dst) in enumerate(((xr, yr), (dr, dyr)))
         ]
 
-    for e in range(min(2, per_tile)):
+    for e in range(per_tile):
         ag_start(e, 0)
 
     block = min(256, rows)
@@ -278,10 +278,6 @@
         @pl.when(s + 1 < hops)
         def _():
             ag_start(e, s + 1)
-
-        @pl.when(jnp.logical_and(s == hops - 1, e + 2 < per_tile))
-        def _():
-            ag_start(e + 2, 0)
 
     lax.fori_loop(0, per_tile * tiles, pack, 0)
 

time: 215 us -> 216 us (level)
  no operation moved by 1% of the time
where the time goes in v3:
time: 216 us
  Pallas kernels  206 us (95%)
  local copies, waits for them, and re-layouts  9.14 us (4%)
    pallas_call x1, Pallas kernels, on_device(): pl.pallas_call(functools.partial(kernel, tiles, blks, per_tile, cap), out...  206 us
    unnamed x18, local copies, waits for them, and re-layouts  8.57 us

profile of v3, /device:TPU:0, one launch (start us, length us, event | category | flops | bytes accessed | tf_op | source)
XLA Modules:
  0.0 215.8 jit_solution(9139595397644085774)
XLA Ops:
  0.6 0.0 copy-start.5
  0.6 0.7 copy-done.5
  1.3 0.6 reshape.15.gain
  1.9 206.0 %shard_map.127 = (bf16[1024,384]{1,0:T(8,128)(2,1)}, f32[2,1024]{1,0:T(2,128)}, bf16[1024,384]{1,0:T(8,128)(2,1)}, f32[4,48,1024]{2,1,0:T(8,128)}, f32[4,48,1024]{2,1,0:T(8,128)}, /*index=5*/f32[4,128,384]{2,1,0:T(8,128)}) custom-call(bf16[1024,384]{1,0:T(8,128)(2,1)} %tok.1, f32[1,384]{1,0:T(1,128)} %reshape.15.gain, s32[2,1024]{1,0:T(2,128)} %bitcast.3, ...), custom_call_target="tpu_custom_call" | custom-call | tf_op jit(solution)/shard_map/pallas_call | solution.py:473
  207.9 0.0 copy-start.4
  207.9 0.0 copy-start.3
  207.9 2.2 %copy.20 = bf16[1024,384]{1,0:T(8,128)(2,1)} copy(bf16[1024,384]{1,0:T(8,128)(2,1)} %get-tuple-element.24) | data formatting | bytes 1572864
  210.0 0.0 copy-done.4
  210.0 0.6 copy.21
  210.6 0.0 copy-done.3
  210.6 0.0 copy-start.2
  210.7 0.9 copy.22
  211.5 0.5 copy-done.2
  212.1 0.0 copy-start.1
  212.1 0.9 copy.23
  212.9 0.5 copy-done.1
  213.5 0.0 copy-start
  213.5 0.9 copy.24
  214.4 0.5 copy-done
  214.9 0.9 copy.25
Async XLA Ops:
  0.6 0.7 copy-start.5
  207.9 2.2 %copy-start.4 = (f32[2,1024]{1,0:T(2,128)S(1)}, f32[2,1024]{1,0:T(2,128)}, u32[]{:S(2)}) copy-start(f32[2,1024]{1,0:T(2,128)} %get-tuple-element.13) | copy-start | bytes 24580
  207.9 2.8 %copy-start.3 = (bf16[1024,384]{1,0:T(8,128)(2,1)S(1)}, bf16[1024,384]{1,0:T(8,128)(2,1)}, u32[]{:S(2)}) copy-start(bf16[1024,384]{1,0:T(8,128)(2,1)} %get-tuple-element.26) | copy-start | bytes 2359300
  210.6 1.4 copy-start.2
  212.1 1.4 copy-start.1
  213.5 1.4 copy-start
